TPU v7x, 32 devices: a whole 2x2x4 slice. The times are simulated.
32 devices in a mesh: dp: 4 (over y, core), tensor: 8 (over z, x).
Axes of the slice: x: 2, y: 2, z: 4, core: 2. Of those that a mesh axis runs over, the one named last changes fastest.
Arguments:
- hidden_in: bfloat16 [3072, 2048], P(('dp', 'tensor')), may hold values from -6 to 6
- norm1_gain: bfloat16 [2048], replicated, may hold values from 0.099609375 to 1.8984375
- norm2_gain: bfloat16 [2048], replicated, may hold values from 0.099609375 to 1.8984375
- w_query: bfloat16 [2048, 2048], P(None, 'tensor'), may hold values from -0.125 to 0.125
- w_keyval: bfloat16 [2048, 256], replicated, may hold values from -0.125 to 0.125
- w_out: bfloat16 [2048, 2048], P('tensor'), may hold values from -0.5 to 0.5
- w_fc: bfloat16 [2048, 8192], P(None, 'tensor'), may hold values from -0.125 to 0.125
- w_proj: bfloat16 [8192, 2048], P('tensor'), may hold values from -0.0625 to 0.0625
- prefix_kv: bfloat16 [4, 4096, 256], P('dp', 'tensor'), may hold values from -320 to 320
- owner_ids: int32 [4], replicated, may hold values from 0 to 3, each once
- segment_ids: int32 [4, 768], P('dp'), may hold values from 0 to 11, never falling along the last dimension, each value on 1 to 192 neighbouring positions
Outputs:
- layer_out: bfloat16 [3072, 2048], P(('dp', 'tensor'))
- attended: bfloat16 [3072, 2048], P(('dp', 'tensor'))
Inputs may be any that keep to these rules, and one draw needn't show every extreme that they name: `owner_ids`: each stored prefix is extended by exactly one group. `segment_ids`: within a group the request ids never fall; every one of the 12 requests has 1 to 192 tokens, and at least one has exactly 192.
All inputs are finite; a program needn't handle non-finite values.
Results may differ from a plain program's by a relative error of at most 0.015.
Values may be sent and summed in bfloat16 or wider, within the bound.
A program may use at most 128 MiB of HBM per device.

v0:
```python
import math
import jax
import jax.numpy as jnp
from jax import lax
from jax.sharding import PartitionSpec as P


def layer_norm(values, scales):
    widened = values.astype(jnp.float32)
    centre = jnp.mean(widened, axis=-1, keepdims=True)
    centred = widened - centre
    variance = jnp.mean(centred * centred, axis=-1, keepdims=True)
    return (centred * lax.rsqrt(variance + 1e-05) * scales.astype(jnp.float32)).astype(jnp.bfloat16)


def attend_block(state_in, queries, key_rows, value_rows, allowed):
    running, totals, weighted = state_in
    scores = jnp.einsum("htd,kd->htk", queries, key_rows, preferred_element_type=jnp.float32)
    if allowed is not None:
        scores = jnp.where(allowed[None], scores, -jnp.inf)
    new_top = jnp.maximum(running, jnp.max(scores, axis=-1))
    factor = jnp.exp(running - new_top)
    probs = jnp.exp(scores - new_top[..., None])
    totals = totals * factor + jnp.sum(probs, axis=-1)
    probs_b = probs.astype(jnp.bfloat16)
    weighted = weighted * factor[..., None] + jnp.einsum(
        "htk,kd->htd", probs_b, value_rows, preferred_element_type=jnp.float32
    )
    return (new_top, totals, weighted)


def local(
    hidden_in,
    norm1_gain,
    norm2_gain,
    w_query,
    w_keyval,
    w_out,
    w_fc,
    w_proj,
    prefix_kv,
    owner_ids,
    segment_ids,
):
    head_size = w_keyval.shape[1] // 2
    query_cols = w_query.shape[1]
    heads_here = query_cols // head_size
    row_len = segment_ids.shape[1]
    q_scale = 1.0 / math.sqrt(head_size)
    w_joint = jnp.concatenate([w_query, w_keyval], axis=1)
    col_scale = jnp.concatenate(
        [jnp.full((query_cols,), q_scale, jnp.float32), jnp.ones((2 * head_size,), jnp.float32)]
    )
    normed = layer_norm(hidden_in, norm1_gain)
    projected = (
        jnp.dot(
            lax.all_gather(normed, "tensor", axis=0, tiled=True),
            w_joint,
            preferred_element_type=jnp.float32,
        )
        * col_scale
    ).astype(jnp.bfloat16)
    group_here = owner_ids[lax.axis_index("dp")]
    fragment = lax.all_gather(prefix_kv, "dp", axis=0, tiled=True)
    span_len = fragment.shape[0]
    match_rows = jnp.arange(span_len, dtype=jnp.int32) == group_here
    cached = jnp.sum(
        jnp.where(match_rows[:, None, None], fragment, jnp.zeros_like(fragment)), axis=0
    )
    queries = projected[:, :query_cols].reshape(row_len, heads_here, head_size).transpose(1, 0, 2)
    suffix_keys = projected[:, query_cols : query_cols + head_size]
    suffix_values = projected[:, query_cols + head_size :]
    request_ids = segment_ids[0]
    positions = jnp.arange(row_len, dtype=jnp.int32)
    allowed = (positions[None, :] <= positions[:, None]) & (
        request_ids[None, :] == request_ids[:, None]
    )
    start_state = (
        jnp.full((heads_here, row_len), -jnp.inf, jnp.float32),
        jnp.zeros((heads_here, row_len), jnp.float32),
        jnp.zeros((heads_here, row_len, head_size), jnp.float32),
    )
    suffix_state = attend_block(start_state, queries, suffix_keys, suffix_values, allowed)
    fragment = lax.all_gather(cached, "tensor", axis=0, tiled=True)
    state_out = suffix_state
    for row_begin in range(0, fragment.shape[0], 1024):
        block_rows = fragment[row_begin : row_begin + 1024]
        state_out = attend_block(
            state_out, queries, block_rows[:, :head_size], block_rows[:, head_size:], None
        )
    running, totals, weighted = state_out
    attn_heads = (
        (weighted / totals[..., None])
        .astype(jnp.bfloat16)
        .transpose(1, 0, 2)
        .reshape(row_len, query_cols)
    )
    term = jnp.dot(attn_heads, w_out, preferred_element_type=jnp.float32)
    attended = lax.psum_scatter(
        term.astype(jnp.bfloat16).astype(jnp.float32).astype(jnp.bfloat16),
        "tensor",
        scatter_dimension=0,
        tiled=True,
    )
    middle = (hidden_in.astype(jnp.float32) + attended.astype(jnp.float32)).astype(jnp.bfloat16)
    normed2 = layer_norm(middle, norm2_gain)
    hidden_act = jax.nn.gelu(
        jnp.dot(
            lax.all_gather(normed2, "tensor", axis=0, tiled=True),
            w_fc,
            preferred_element_type=jnp.float32,
        ),
        approximate=True,
    ).astype(jnp.bfloat16)
    term = jnp.dot(hidden_act, w_proj, preferred_element_type=jnp.float32)
    mlp_sum = lax.psum_scatter(
        term.astype(jnp.bfloat16).astype(jnp.float32).astype(jnp.bfloat16),
        "tensor",
        scatter_dimension=0,
        tiled=True,
    ).astype(jnp.float32)
    layer_out = (middle.astype(jnp.float32) + mlp_sum).astype(jnp.bfloat16)
    return (layer_out, attended)


def solution(mesh):
    return jax.shard_map(
        local,
        mesh=mesh,
        in_specs=(
            P(("dp", "tensor"), None),
            P(),
            P(),
            P(None, "tensor"),
            P(),
            P("tensor", None),
            P(None, "tensor"),
            P("tensor", None),
            P("dp", "tensor", None),
            P(),
            P("dp", None),
        ),
        out_specs=(P(("dp", "tensor"), None), P(("dp", "tensor"), None)),
        check_vma=False,
    )
```

profile of v0, /device:TPU:0, one launch (start us, length us, event | category | flops | bytes accessed | tf_op | source)
XLA Modules:
  0.0 392.4 jit_solution(12325680166661259745)
XLA Ops:
  8.7 1.1 convert_reduce_fusion.1
  9.8 1.3 fusion.102
  11.1 2.0 fusion.104
  13.2 1.2 dynamic_slice.3
  15.1 13.9 %all-gather.7.cloned.1.call-done = bf16[4,512,256]{2,1,0:T(8,128)(2,1)} async-done(((bf16[1,512,256]{2,1,0:T(8,128)(2,1)}), bf16[4,512,256]{2,1,0:T(8,128)(2,1)}) %all-gather.7.cloned.1.call-update) | async-done | bytes 1048592 | tf_op jit(solution)/shard_map/all_gather | solution.py:64
  29.1 2.2 select_reduce_fusion.1
  31.4 0.7 reduce.1
  32.4 59.8 %all-gather.5.cloned.1.call-done = bf16[768,2048]{1,0:T(8,128)(2,1)} async-done(((bf16[96,2048]{1,0:T(8,128)(2,1)}), bf16[768,2048]{1,0:T(8,128)(2,1)}) %all-gather.5.cloned.1.call-update) | async-done | bytes 3145744 | tf_op jit(solution)/shard_map/all_gather | solution.py:57
  92.3 4.0 %multiply_convert_fusion = bf16[768,512]{0,1:T(8,128)(2,1)S(1)} fusion(bf16[768,2048]{1,0:T(8,128)(2,1)} %all-gather.5.cloned.1.call-done, bf16[2048,256]{1,0:T(8,128)(2,1)S(1)} %copy-done.5, bf16[2048,256]{1,0:T(8,128)(2,1)} %param.14, f32[512]{0:T(512)S(1)} %copy-done.6), kind=kOutput, calls=%fused_computation.49 | convolution fusion | flops 1615593472 | bytes 6031360 | tf_op jit(solution)/shard_map/dot_general | solution.py:56
  96.6 1.0 select_reduce_fusion
  97.6 2.1 copy-done.1
  99.7 0.9 fusion.8
  100.6 42.3 %all-gather.9.cloned.1.call-done = bf16[4096,256]{1,0:T(8,128)(2,1)} async-done(((bf16[512,256]{1,0:T(8,128)(2,1)}), bf16[4096,256]{1,0:T(8,128)(2,1)}) %all-gather.9.cloned.1.call-update) | async-done | bytes 2097168 | tf_op jit(solution)/shard_map/all_gather | solution.py:84
  142.9 2.2 fusion.136
  145.1 1.1 fusion.137
  146.2 1.1 fusion.138
  147.3 1.1 fusion.135
  148.3 2.6 fusion
  150.9 2.4 fusion.4
  153.4 1.3 fusion.50
  154.7 1.3 fusion.53
  155.9 1.3 fusion.56
  157.2 1.3 fusion.59
  158.5 1.6 fusion.92
  160.1 2.7 convolution_convert_fusion.1
  162.9 72.9 %reduce-scatter.3.cloned.1.call-done = bf16[96,2048]{1,0:T(8,128)(2,1)} async-done(((bf16[768,2048]{1,0:T(8,128)(2,1)}), bf16[96,2048]{1,0:T(8,128)(2,1)}) %reduce-scatter.3.cloned.1.call-update) | async-done | bytes 393232 | tf_op jit(solution)/shard_map/reduce_scatter | solution.py:99
  235.8 1.2 convert_reduce_fusion
  237.3 1.0 fusion.101
  238.4 59.6 %all-gather.11.cloned.1.call-done = bf16[768,2048]{1,0:T(8,128)(2,1)} async-done(((bf16[96,2048]{1,0:T(8,128)(2,1)}), bf16[768,2048]{1,0:T(8,128)(2,1)}) %all-gather.11.cloned.1.call-update) | async-done | bytes 3145744 | tf_op jit(solution)/shard_map/all_gather | solution.py:109
  298.0 12.5 %convolution_convert_fusion = bf16[768,2048]{1,0:T(8,128)(2,1)} fusion(bf16[1024,2048]{1,0:T(8,128)(2,1)} %param.18, bf16[768,2048]{1,0:T(8,128)(2,1)} %all-gather.11.cloned.1.call-done, bf16[2048,1024]{1,0:T(8,128)(2,1)} %param.17), kind=kOutput, calls=%fused_computation.17 | convolution fusion | flops 6451101696 | bytes 14680064 | tf_op jit(solution)/shard_map/dot_general | solution.py:115
  310.6 73.2 %reduce-scatter.5.cloned.1.call-done = bf16[96,2048]{1,0:T(8,128)(2,1)} async-done(((bf16[768,2048]{1,0:T(8,128)(2,1)}), bf16[96,2048]{1,0:T(8,128)(2,1)}) %reduce-scatter.5.cloned.1.call-update) | async-done | bytes 393232 | tf_op jit(solution)/shard_map/reduce_scatter | solution.py:116
  383.8 1.8 fusion.106
  (43 shorter events, 3.4 us)
Async XLA Ops:
  7.2 152.9 %copy-start = (bf16[256,2048]{1,0:T(8,128)(2,1)S(1)}, bf16[256,2048]{1,0:T(8,128)(2,1)}, u32[]{:S(2)}) copy-start(bf16[256,2048]{1,0:T(8,128)(2,1)} %param.16) | copy-start | bytes 3145732
  7.2 85.1 %copy-start.6 = (f32[512]{0:T(512)S(1)}, f32[512]{0:T(512)}, u32[]{:S(2)}) copy-start(f32[512]{0:T(512)} %constant.8.clone.1) | copy-start | bytes 6148
  7.2 85.1 %copy-start.5 = (bf16[2048,256]{1,0:T(8,128)(2,1)S(1)}, bf16[2048,256]{1,0:T(8,128)(2,1)}, u32[]{:S(2)}) copy-start(bf16[2048,256]{1,0:T(8,128)(2,1)} %param.15) | copy-start | bytes 3145732
  7.2 21.9 %all-gather.7.cloned.1.call-start = ((), (), s32[]{:S(2)}) async-start(), calls=%async_computation.3 | async-start | bytes 1310720 | tf_op jit(solution)/shard_map/all_gather | solution.py:64
  7.9 84.4 %all-gather.5.cloned.1.call-start = ((), (), s32[]{:S(2)}) async-start(), calls=%async_computation.2 | async-start | bytes 3538944 | tf_op jit(solution)/shard_map/all_gather | solution.py:57
  13.2 129.8 %all-gather.9.cloned.1.call-start = ((), (), s32[]{:S(2)}) async-start(), calls=%async_computation.4 | async-start | bytes 2359296 | tf_op jit(solution)/shard_map/all_gather | solution.py:84
  31.3 204.5 %reduce-scatter.3.cloned.1.call-start = ((), (), s32[]{:S(2)}) async-start(), calls=%async_computation.5 | async-start | bytes 3538944 | tf_op jit(solution)/shard_map/reduce_scatter | solution.py:99
  97.6 2.1 copy-start.1
  142.9 2.2 copy-start.3
  154.7 3.8 slice-start
  155.9 2.5 slice-start.1
  160.1 2.8 copy-start.4
  160.1 75.7 %copy-start.2 = (bf16[96,2048]{1,0:T(8,128)(2,1)S(1)}, bf16[96,2048]{1,0:T(8,128)(2,1)}, u32[]{:S(2)}) copy-start(bf16[96,2048]{1,0:T(8,128)(2,1)} %param.11) | copy-start | bytes 1179652
  162.8 135.2 %all-gather.11.cloned.1.call-start = ((), (), s32[]{:S(2)}) async-start(), calls=%async_computation.6 | async-start | bytes 3538944 | tf_op jit(solution)/shard_map/all_gather | solution.py:109
  238.4 145.4 %reduce-scatter.5.cloned.1.call-start = ((), (), s32[]{:S(2)}) async-start(), calls=%async_computation.7 | async-start | bytes 3538944 | tf_op jit(solution)/shard_map/reduce_scatter | solution.py:116
Sparse Core Ops, SparseCore 0:
  9.6 19.4 all-gather.6
  31.8 60.4 all-gather.4
  95.0 47.9 all-gather.8
  162.9 72.8 reduce-scatter.2
  238.5 59.5 all-gather.10
  310.7 73.0 reduce-scatter.4
where the time goes:
time: 393 us; the launch traced here: 392 us
  waiting for transfers between devices  323 us (82%)
  matrix products  32.1 us (8%)
  other arithmetic  19.4 us (5%)
  between operations  14.4 us (4%)
    reduce_scatter x2, waiting for transfers between devices, local(): lax.psum_scatter(term.astype(jnp.bfloat16).astype(jnp.float32).astype(jnp...  146 us
    all_gather x1, waiting for transfers between devices, local(): lax.all_gather(normed, 'tensor', axis=0, tiled=True)  59.8 us
    all_gather x1, waiting for transfers between devices, local(): lax.all_gather(normed2, 'tensor', axis=0, tiled=True)  59.6 us
    all_gather x1, waiting for transfers between devices, local(): fragment = lax.all_gather(cached, 'tensor', axis=0, tiled=True)  42.3 us
    all_gather x1, waiting for transfers between devices, local(): fragment = lax.all_gather(prefix_kv, 'dp', axis=0, tiled=True)  13.9 us
    dot_general x1, matrix products, local(): term = jnp.dot(hidden_act, w_proj, preferred_element_type=jnp.float32)  12.5 us
  transfers between devices with their start and end apart: 6, of which 6 were waited for; matrix products, arithmetic and copies ran while one was open for 4% of the time, Pallas kernels for 0%

commit v1 on v0

--- a/solution.py
+++ b/solution.py
@@ -3,6 +3,19 @@
 import jax.numpy as jnp
 from jax import lax
 from jax.sharding import PartitionSpec as P
+
+
+def collect(x, axis, dim):
+    ways = lax.axis_size(axis)
+    up = [(d, (d + 1) % ways) for d in range(ways)]
+    down = [(d, (d - 1) % ways) for d in range(ways)]
+    earlier, later = ([x], [x])
+    for _ in range(ways // 2):
+        earlier.append(lax.ppermute(earlier[-1], axis, up))
+    for _ in range((ways - 1) // 2):
+        later.append(lax.ppermute(later[-1], axis, down))
+    line = jnp.concatenate([*earlier[::-1], *later[1:]], axis=dim)
+    return jnp.roll(line, (lax.axis_index(axis) - ways // 2) * x.shape[dim], axis=dim)
 
 
 def layer_norm(values, scales):
@@ -61,7 +74,7 @@
         * col_scale
     ).astype(jnp.bfloat16)
     group_here = owner_ids[lax.axis_index("dp")]
-    fragment = lax.all_gather(prefix_kv, "dp", axis=0, tiled=True)
+    fragment = collect(prefix_kv, "dp", 0)
     span_len = fragment.shape[0]
     match_rows = jnp.arange(span_len, dtype=jnp.int32) == group_here
     cached = jnp.sum(

time: 393 us -> 376 us (0.957)
  waiting for transfers between devices: 323 us -> 305 us
    all_gather x1 -> x0, waiting for transfers between devices: 13.9 us -> none  [local(): fragment = lax.all_gather(prefix_kv, 'dp', axis=0, tiled=True)]
    all_gather x1, waiting for transfers between devices: 59.8 us -> 46.4 us  [local(): lax.all_gather(normed, 'tensor', axis=0, tiled=True)]
    ppermute x0 -> x3, waiting for transfers between devices: none -> 11 us  [the longest x2 8.35 us: collect(): earlier.append(lax.ppermute(earlier[-1], axis, up))]
  transfers between devices with their start and end apart: 6 -> 8, of which waited for: 6 -> 8; matrix products, arithmetic and copies ran while one was open for 4% -> 3% of each run, Pallas kernels for 0% -> 0%
where the time goes in v1:
time: 376 us
  waiting for transfers between devices  305 us (81%)
  matrix products  32.2 us (9%)
  other arithmetic  17.7 us (5%)
  between operations  14.1 us (4%)
  local copies, waits for them, and re-layouts  4.42 us (1%)
    reduce_scatter x2, waiting for transfers between devices, local(): lax.psum_scatter(term.astype(jnp.bfloat16).astype(jnp.float32).astype(jnp...  145 us
    all_gather x1, waiting for transfers between devices, local(): lax.all_gather(normed2, 'tensor', axis=0, tiled=True)  59.6 us
    all_gather x1, waiting for transfers between devices, local(): lax.all_gather(normed, 'tensor', axis=0, tiled=True)  46.4 us
    all_gather x1, waiting for transfers between devices, local(): fragment = lax.all_gather(cached, 'tensor', axis=0, tiled=True)  42.3 us
    dot_general x1, matrix products, local(): term = jnp.dot(hidden_act, w_proj, preferred_element_type=jnp.float32)  12.6 us
    ppermute x2, waiting for transfers between devices, collect(): earlier.append(lax.ppermute(earlier[-1], axis, up))  8.35 us
  transfers between devices with their start and end apart: 8, of which 8 were waited for; matrix products, arithmetic and copies ran while one was open for 3% of the time, Pallas kernels for 0%

profile of v1, /device:TPU:0, one launch (start us, length us, event | category | flops | bytes accessed | tf_op | source)
XLA Modules:
  0.0 375.8 jit_solution(14206177625585959482)
XLA Ops:
  7.2 1.3 convert_reduce_fusion.1
  8.5 1.3 fusion.102
  10.5 2.0 fusion.104
  13.1 6.2 %collective-permute-done = bf16[1,512,256]{2,1,0:T(8,128)(2,1)S(1)} collective-permute-done((bf16[1,512,256]{2,1,0:T(8,128)(2,1)}, bf16[1,512,256]{2,1,0:T(8,128)(2,1)S(1)}, u32[]{:S(2)}, u32[]{:S(2)}) %collective-permute-start) | collective-permute-done | bytes 262176 | tf_op jit(solution)/shard_map/ppermute | solution.py:14
  19.3 1.7 collective-permute-start.2
  21.1 1.2 dynamic_slice.7
  23.0 2.1 collective-permute-done.1
  25.2 2.6 collective-permute-done.2
  28.0 1.0 select_reduce_fusion.1
  29.5 46.4 %all-gather.4.cloned.1.call-done = bf16[768,2048]{1,0:T(8,128)(2,1)} async-done(((bf16[96,2048]{1,0:T(8,128)(2,1)}), bf16[768,2048]{1,0:T(8,128)(2,1)}) %all-gather.4.cloned.1.call-update) | async-done | bytes 3145744 | tf_op jit(solution)/shard_map/all_gather | solution.py:70
  75.8 4.0 %multiply_convert_fusion = bf16[768,512]{0,1:T(8,128)(2,1)S(1)} fusion(bf16[768,2048]{1,0:T(8,128)(2,1)} %all-gather.4.cloned.1.call-done, bf16[2048,256]{1,0:T(8,128)(2,1)S(1)} %copy-done.8, bf16[2048,256]{1,0:T(8,128)(2,1)} %param.14, f32[512]{0:T(512)S(1)} %copy-done.9), kind=kOutput, calls=%fused_computation.49 | convolution fusion | flops 1615593472 | bytes 6031360 | tf_op jit(solution)/shard_map/dot_general | solution.py:69
  81.1 2.1 copy-done.2
  84.2 42.3 %all-gather.6.cloned.1.call-done = bf16[4096,256]{1,0:T(8,128)(2,1)} async-done(((bf16[512,256]{1,0:T(8,128)(2,1)}), bf16[4096,256]{1,0:T(8,128)(2,1)}) %all-gather.6.cloned.1.call-update) | async-done | bytes 2097168 | tf_op jit(solution)/shard_map/all_gather | solution.py:97
  126.5 2.2 fusion.136
  128.6 1.1 fusion.137
  129.7 1.1 fusion.138
  130.8 1.1 fusion.135
  131.9 2.7 fusion
  134.6 2.4 fusion.4
  137.0 1.3 fusion.50
  138.3 1.3 fusion.53
  139.6 1.3 fusion.56
  140.9 1.3 fusion.59
  142.1 1.6 fusion.92
  143.7 2.7 convolution_convert_fusion.1
  147.1 72.4 %reduce-scatter.3.cloned.1.call-done = bf16[96,2048]{1,0:T(8,128)(2,1)} async-done(((bf16[768,2048]{1,0:T(8,128)(2,1)}), bf16[96,2048]{1,0:T(8,128)(2,1)}) %reduce-scatter.3.cloned.1.call-update) | async-done | bytes 393232 | tf_op jit(solution)/shard_map/reduce_scatter | solution.py:112
  219.5 1.2 convert_reduce_fusion
  221.0 1.0 fusion.101
  222.1 59.6 %all-gather.8.cloned.1.call-done = bf16[768,2048]{1,0:T(8,128)(2,1)} async-done(((bf16[96,2048]{1,0:T(8,128)(2,1)}), bf16[768,2048]{1,0:T(8,128)(2,1)}) %all-gather.8.cloned.1.call-update) | async-done | bytes 3145744 | tf_op jit(solution)/shard_map/all_gather | solution.py:122
  281.7 12.6 %convolution_convert_fusion = bf16[768,2048]{1,0:T(8,128)(2,1)} fusion(bf16[1024,2048]{1,0:T(8,128)(2,1)} %param.18, bf16[768,2048]{1,0:T(8,128)(2,1)} %all-gather.8.cloned.1.call-done, bf16[2048,1024]{1,0:T(8,128)(2,1)} %param.17), kind=kOutput, calls=%fused_computation.17 | convolution fusion | flops 6451101696 | bytes 14680064 | tf_op jit(solution)/shard_map/dot_general | solution.py:128
  294.3 73.1 %reduce-scatter.5.cloned.1.call-done = bf16[96,2048]{1,0:T(8,128)(2,1)} async-done(((bf16[768,2048]{1,0:T(8,128)(2,1)}), bf16[96,2048]{1,0:T(8,128)(2,1)}) %reduce-scatter.5.cloned.1.call-update) | async-done | bytes 393232 | tf_op jit(solution)/shard_map/reduce_scatter | solution.py:129
  367.4 1.8 fusion.106
  (60 shorter events, 5.9 us)
Async XLA Ops:
  7.2 136.6 %copy-start = (bf16[256,2048]{1,0:T(8,128)(2,1)S(1)}, bf16[256,2048]{1,0:T(8,128)(2,1)}, u32[]{:S(2)}) copy-start(bf16[256,2048]{1,0:T(8,128)(2,1)} %param.16) | copy-start | bytes 3145732
  7.2 18.0 %copy-start.5 = (bf16[1,512,256]{2,1,0:T(8,128)(2,1)S(1)}, bf16[1,512,256]{2,1,0:T(8,128)(2,1)}, u32[]{:S(2)}) copy-start(bf16[1,512,256]{2,1,0:T(8,128)(2,1)} %param.19) | copy-start | bytes 786436
  7.2 68.6 %all-gather.4.cloned.1.call-start = ((), (), s32[]{:S(2)}) async-start(), calls=%async_computation.2 | async-start | bytes 3538944 | tf_op jit(solution)/shard_map/all_gather | solution.py:70
  12.5 16.6 %copy-start.7 = (s32[1,768]{1,0:T(1,128)S(1)}, s32[1,768]{1,0:T(1,128)}, u32[]{:S(2)}) copy-start(s32[1,768]{1,0:T(1,128)} %param.21) | copy-start | bytes 9220
  12.5 113.9 %all-gather.6.cloned.1.call-start = ((), (), s32[]{:S(2)}) async-start(), calls=%async_computation.3 | async-start | bytes 2359296 | tf_op jit(solution)/shard_map/all_gather | solution.py:97
  12.6 6.7 %collective-permute-start = (bf16[1,512,256]{2,1,0:T(8,128)(2,1)}, bf16[1,512,256]{2,1,0:T(8,128)(2,1)S(1)}, u32[]{:S(2)}, u32[]{:S(2)}) collective-permute-start(bf16[1,512,256]{2,1,0:T(8,128)(2,1)} %param.19), channel_id=1, source_target_pairs={{0,8},{8,16},{16,24},{24,0},{1,9},{9,17},{17,25},{25,1},{2,10},{10... | collective-permute-start | bytes 786440 | tf_op jit(solution)/shard_map/ppermute | solution.py:14
  19.3 5.8 %collective-permute-start.1 = (bf16[1,512,256]{2,1,0:T(8,128)(2,1)S(1)}, bf16[1,512,256]{2,1,0:T(8,128)(2,1)S(1)}, u32[]{:S(2)}, u32[]{:S(2)}) collective-permute-start(bf16[1,512,256]{2,1,0:T(8,128)(2,1)S(1)} %collective-permute-done), channel_id=1, source_target_pairs={{0,8},{8,16},{16,24},{24,0},{1,9},{9,17},{17,25},{25,1},{2,10},{10... | collective-permute-start | bytes 786440 | tf_op jit(solution)/shard_map/ppermute | solution.py:14
  19.3 8.5 %collective-permute-start.2 = (bf16[1,512,256]{2,1,0:T(8,128)(2,1)}, bf16[1,512,256]{2,1,0:T(8,128)(2,1)S(1)}, u32[]{:S(2)}, u32[]{:S(2)}) collective-permute-start(bf16[1,512,256]{2,1,0:T(8,128)(2,1)} %param.19), channel_id=1, source_target_pairs={{0,24},{8,0},{16,8},{24,16},{1,25},{9,1},{17,9},{25,17},{2,26},{10... | collective-permute-start | bytes 786440 | tf_op jit(solution)/shard_map/ppermute | solution.py:16
  23.0 52.9 %copy-start.8 = (bf16[2048,256]{1,0:T(8,128)(2,1)S(1)}, bf16[2048,256]{1,0:T(8,128)(2,1)}, u32[]{:S(2)}) copy-start(bf16[2048,256]{1,0:T(8,128)(2,1)} %param.15) | copy-start | bytes 3145732
  23.0 52.9 %copy-start.9 = (f32[512]{0:T(512)S(1)}, f32[512]{0:T(512)}, u32[]{:S(2)}) copy-start(f32[512]{0:T(512)} %constant.49.clone.1) | copy-start | bytes 6148
  29.0 190.5 %reduce-scatter.3.cloned.1.call-start = ((), (), s32[]{:S(2)}) async-start(), calls=%async_computation.4 | async-start | bytes 3538944 | tf_op jit(solution)/shard_map/reduce_scatter | solution.py:112
  81.1 2.1 copy-start.2
  126.5 2.2 copy-start.4
  138.3 3.8 %slice-start = ((s8[4718592]{0:T(1024)(128)(4,1)}), s8[524288]{0:T(1024)(128)(4,1)S(1)}, s32[]{:S(2)}) async-start(s8[4718592]{0:T(1024)(128)(4,1)} %bitcast.196), calls=%async_computation.7 | async-start | bytes 1048576
  139.6 2.5 slice-start.1
  146.4 0.7 copy-start.6
  146.4 73.1 %copy-start.3 = (bf16[96,2048]{1,0:T(8,128)(2,1)S(1)}, bf16[96,2048]{1,0:T(8,128)(2,1)}, u32[]{:S(2)}) copy-start(bf16[96,2048]{1,0:T(8,128)(2,1)} %param.11) | copy-start | bytes 1179652
  146.4 135.3 %all-gather.8.cloned.1.call-start = ((), (), s32[]{:S(2)}) async-start(), calls=%async_computation.5 | async-start | bytes 3538944 | tf_op jit(solution)/shard_map/all_gather | solution.py:122
  222.1 145.3 %reduce-scatter.5.cloned.1.call-start = ((), (), s32[]{:S(2)}) async-start(), calls=%async_computation.6 | async-start | bytes 3538944 | tf_op jit(solution)/shard_map/reduce_scatter | solution.py:129
  281.7 87.5 %copy-start.1 = (bf16[256,2048]{1,0:T(8,128)(2,1)S(1)}, bf16[256,2048]{1,0:T(8,128)(2,1)}, u32[]{:S(2)}) copy-start(bf16[256,2048]{1,0:T(8,128)(2,1)} %param.16) | copy-start | bytes 3145732
Sparse Core Ops, SparseCore 0:
  12.7 63.1 all-gather.3
  78.5 47.9 all-gather.5
  146.6 72.8 reduce-scatter.2
  222.2 59.5 all-gather.7
  294.4 72.8 reduce-scatter.4
